TPU v7x, 256 devices: a whole 4x4x8 slice. The times are simulated.
256 devices in a mesh: section: 4 (over y), chan: 64 (over x, z, core).
Axes of the slice: x: 4, y: 4, z: 8, core: 2. Of those that a mesh axis runs over, the one named last changes fastest.
Arguments:
- voltages: bfloat16 [2, 1024, 16, 4096], P(None, 'chan', 'section'), may hold values from -6 to 6
- coefficients: float32 [4, 4096], replicated, may hold values from -0.046875 to 0.046875
- tile_order: int32 [64, 36], P('chan'), may hold values from 0 to 35, each once within a row
- steer_table: bfloat16 [256, 2, 512], replicated, may hold values from -0.1875 to 0.1875
- beam_index: int32 [256, 64], P(None, 'chan'), may hold values from 0 to 255
Outputs:
- visibility: float32 [64, 36, 2, 128, 128], P('chan', 'section')
- beam_power: float32 [2, 256, 16, 4096], P(None, None, 'section', 'chan')
Inputs may be any that keep to these rules, and one draw needn't show every extreme that they name: Row g of tile_order lists each of the 36 work items of channel column g exactly once.
All inputs are finite; a program needn't handle non-finite values.
Results may differ from a plain program's by a relative error of at most 0.0029.
Values may be sent and summed in bfloat16 or wider, within the bound.
A program may use at most 64 MiB of HBM per device.

v0:
```python
import math
import jax
import jax.numpy as jnp
from jax import lax
from jax.sharding import PartitionSpec as P

STATIONS = 512
INPUTS = 1024
NA = 64
NB = 64
AVG = 64
TB = 128
PAIRS = 36
NBEAM = 256


def shifted(value, axis, by):
    devices = lax.axis_size(axis)
    pairs = [(i, i + by) for i in range(devices) if 0 <= i + by < devices]
    return lax.ppermute(value, axis, pairs)


def dft_table(length):
    counter = lax.iota(jnp.int32, length)
    phases = counter[:, None] * counter[None, :] % length
    angles = 2.0 * math.pi / length * phases.astype(jnp.float32)
    cosine = jnp.cos(angles)
    sine_part = jnp.sin(angles)
    return jnp.stack([jnp.stack([cosine, -sine_part]), jnp.stack([sine_part, cosine])])


def channelize(filtered):
    spectra_count = filtered.shape[1]
    length = NA * NB
    blocks = filtered.reshape(2, spectra_count, NA, NB)
    section_one = jnp.einsum("qmab,qrac->rmcb", blocks, dft_table(NA), precision=lax.Precision.HIGH)
    row_index = lax.iota(jnp.int32, NA)
    col_index = lax.iota(jnp.int32, NB)
    angles = (
        2.0
        * math.pi
        / length
        * (row_index[:, None] * col_index[None, :] % length).astype(jnp.float32)
    )
    cosine = jnp.cos(angles)
    sine_part = jnp.sin(angles)
    turned_real = section_one[0] * cosine + section_one[1] * sine_part
    turned_imag = section_one[1] * cosine - section_one[0] * sine_part
    twisted = jnp.stack([turned_real, turned_imag])
    section_two = jnp.einsum(
        "rmcb,rsbd->smdc", twisted, dft_table(NB), precision=lax.Precision.HIGH
    )
    return section_two.reshape(2, spectra_count, length)


def pair_products(spectra, work_items):
    tile_count = INPUTS // TB
    local_channel = work_items // PAIRS
    pair_number = work_items % PAIRS
    tile_ids = lax.iota(jnp.int32, tile_count)
    first_pairs = tile_ids * (tile_ids + 1) // 2
    row_tiles = (
        jnp.sum((first_pairs[None, :] <= pair_number[:, None]).astype(jnp.int32), axis=1) - 1
    )
    col_tiles = pair_number - row_tiles * (row_tiles + 1) // 2
    frame_count = spectra.shape[2]
    channel_groups = spectra.shape[3] // AVG
    blocks = spectra.reshape(2, tile_count, TB, frame_count, channel_groups, AVG)
    tile_table = jnp.transpose(blocks, (1, 4, 0, 2, 3, 5)).reshape(
        tile_count * channel_groups, 2, TB, frame_count * AVG
    )
    row_block = jnp.take(tile_table, row_tiles * channel_groups + local_channel, axis=0)
    col_block = jnp.take(tile_table, col_tiles * channel_groups + local_channel, axis=0)
    swapped = jnp.stack([row_block[:, 1], -row_block[:, 0]], axis=1)
    numbers = (((1, 3), (1, 3)), ((0,), (0,)))
    real_part = lax.dot_general(row_block, col_block, numbers, preferred_element_type=jnp.float32)
    imag_part = lax.dot_general(swapped, col_block, numbers, preferred_element_type=jnp.float32)
    return jnp.stack([real_part, imag_part], axis=1)


def shards(voltages, coefficients, tile_order, steer_table, beam_index):
    section_count = lax.axis_size("section")
    inputs_dev = voltages.shape[1]
    frames_dev = voltages.shape[2]
    tap_count = coefficients.shape[0]
    history = shifted(voltages[:, :, frames_dev - (tap_count - 1) :, :], "section", 1)
    extended = jnp.concatenate([history, voltages], axis=2).astype(jnp.float32)
    filtered = jnp.zeros(voltages.shape, jnp.float32)
    for tap_index in range(tap_count):
        offset = tap_count - 1 - tap_index
        filtered = (
            filtered + coefficients[tap_index] * extended[:, :, offset : offset + frames_dev, :]
        )
    spectra = (
        channelize(filtered.reshape(2, inputs_dev * frames_dev, NA * NB))
        .reshape(voltages.shape)
        .astype(jnp.bfloat16)
    )
    weights = steer_table[beam_index]
    out_dev = beam_index.shape[1]
    shard_piece = lax.all_to_all(spectra, "chan", split_axis=3, concat_axis=1, tiled=True)
    frame_count = shard_piece.shape[2]
    grouped = shard_piece.reshape(2, STATIONS, 2, frame_count, out_dev, AVG)
    product = lax.dot_general(
        weights, grouped, (((3,), (1,)), ((1,), (4,))), preferred_element_type=jnp.float32
    )
    real_part = product[:, :, 0, 0] - product[:, :, 1, 1]
    imag_part = product[:, :, 0, 1] + product[:, :, 1, 0]
    beam_energy = real_part * real_part + imag_part * imag_part
    beam_power = jnp.transpose(beam_energy, (2, 1, 3, 0, 4)).reshape(
        2, NBEAM, frame_count, out_dev * AVG
    )
    column_items = tile_order[0]
    items_dev = column_items.shape[0] // section_count
    mean_factor = 1.0 / (frames_dev * section_count * AVG)
    own_items = lax.dynamic_slice_in_dim(
        column_items, lax.axis_index("section") * items_dev, items_dev
    )
    totals = pair_products(lax.all_gather(shard_piece, "section", axis=2, tiled=True), own_items)
    visibility = (totals * mean_factor)[None]
    return (visibility, beam_power)


def solution(mesh):
    placed = (P(None, "chan", "section", None), P(), P("chan", None), P(), P(None, "chan"))
    return jax.shard_map(
        shards,
        mesh=mesh,
        in_specs=placed,
        out_specs=(P("chan", "section", None, None, None), P(None, None, "section", "chan")),
        check_vma=False,
    )
```

profile of v0, /device:TPU:1, one launch (start us, length us, event | category | flops | bytes accessed | tf_op | source)
XLA Modules:
  0.0 257.8 jit_solution(14299678543089905093)
XLA Ops:
  7.2 1.9 slice.54
  9.7 4.1 %collective-permute-start = (bf16[2,16,3,4096]{3,1,2,0:T(8,128)(2,1)S(1)}, bf16[2,16,3,4096]{3,1,2,0:T(8,128)(2,1)S(1)}, u32[]{:S(2)}, u32[]{:S(2)}) collective-permute-start(bf16[2,16,3,4096]{3,1,2,0:T(8,128)(2,1)S(1)} %copy.79), channel_id=1, source_target_pairs={{0,64},{64,128},{128,192},{1,65},{65,129},{129,193},{2,66},{66,130... | collective-permute-start | bytes 2359304 | tf_op jit(solution)/shard_map/ppermute | solution.py:20
  14.4 15.6 %collective-permute-done = bf16[2,16,3,4096]{3,1,2,0:T(8,128)(2,1)S(1)} collective-permute-done((bf16[2,16,3,4096]{3,1,2,0:T(8,128)(2,1)S(1)}, bf16[2,16,3,4096]{3,1,2,0:T(8,128)(2,1)S(1)}, u32[]{:S(2)}, u32[]{:S(2)}) %collective-permute-start) | collective-permute-done | bytes 786464 | tf_op jit(solution)/shard_map/ppermute | solution.py:20
  31.7 1.8 fusion.14
  33.5 3.3 %reshape_reshape.4 = f32[2,64,64,64]{3,2,1,0:T(8,128)} reshape(f32[2,16,4,4096]{3,2,1,0:T(4,128)S(1)} %fusion.14) | data formatting | bytes 4194304 | tf_op jit(solution)/shard_map/reshape;reshape | solution.py:35
  36.9 4.2 %fusion.10 = f32[2,64,64,64]{3,2,1,0:T(8,128)S(1)} fusion(f32[2,64,64,64]{3,2,1,0:T(8,128)} %reshape_reshape.4, f32[1,2,64,64]{2,3,0,1:T(8,128)S(1)} %get-tuple-element.27, f32[1,2,64,64]{2,3,0,1:T(8,128)S(1)} %get-tuple-element.26), kind=kOutput, calls=%fused_computation.18 | convolution fusion | flops 402669568 | bytes 4259840 | tf_op jit(solution)/shard_map/qmab,qrac->rmcb/dot_general | solution.py:36
  42.0 3.3 %fusion.13 = bf16[2,64,64,64]{3,2,1,0:T(8,128)(2,1)S(1)} fusion(f32[1,2,64,64]{2,3,0,1:T(8,128)S(1)} %get-tuple-element.27, f32[1,2,64,64]{2,3,0,1:T(8,128)S(1)} %get-tuple-element.26, f32[1,64,64,64]{3,2,1,0:T(8,128)S(1)} %get-tuple-element.21, f32[1,64,64,64]{3,2,1,0:T(8,128)S(1)} %get-tuple-element.20), kind=kOutput, calls=%fused_computation.19 | convolution fusion | flops 403718144 | bytes 3211264 | tf_op jit(solution)/shard_map/rmcb,rsbd->smdc/dot_general | solution.py:50
  45.3 2.2 convert_element_type.61
  47.5 12.0 %copy.55 = bf16[2,16,4,4096]{1,2,0,3:T(4,128)(2,1)} copy(bf16[2,16,4,4096]{3,2,1,0:T(4,128)(2,1)} %convert_element_type.61) | data formatting | bytes 2097152 | tf_op jit(solution)/shard_map/convert_element_type | solution.py:97
  59.5 11.9 %reshape.317 = bf16[64,2,4096]{2,1,0:T(2,128)(2,1)S(1)} reshape(bf16[4096,2,4,16]{3,2,1,0:T(4,128)(2,1)} %bitcast.95) | data formatting | bytes 2097152
  71.4 41.3 %all_to_all.18 = bf16[64,2,4096]{2,1,0:T(2,128)(2,1)S(1)} all-to-all(bf16[64,2,4096]{2,1,0:T(2,128)(2,1)S(1)} %reshape.317), channel_id=1, replica_groups=mesh['section'=4,'chan'=64] {'chan'}, dimensions={0} | all-to-all | bytes 2097152 | tf_op jit(solution)/shard_map/all_to_all | solution.py:101
  112.7 7.5 %reshape.318 = bf16[4096,2,4,16]{3,2,1,0:T(4,128)(2,1)} reshape(bf16[64,2,4096]{2,1,0:T(2,128)(2,1)S(1)} %all_to_all.18) | data formatting | bytes 2097152
  120.3 11.4 %copy.75 = bf16[2,16,4,64,64]{4,1,3,2,0:T(8,128)(2,1)} copy(bf16[2,16,4,64,64]{1,2,0,4,3:T(4,128)(2,1)} %bitcast.94) | data formatting | bytes 2097152 | tf_op jit(solution)/shard_map/all_to_all | solution.py:101
  131.7 1.7 gather_fusion
  133.9 3.5 %copy.64 = bf16[2,512,2,4,64]{1,4,3,2,0:T(8,128)(2,1)} copy(bf16[2,512,2,4,64]{4,2,1,3,0:T(2,128)(2,1)S(1)} %bitcast.97) | data formatting | bytes 2097152 | tf_op jit(solution)/shard_map/reshape.8
  137.4 2.0 convolution_bitcast_fusion
  140.3 74.9 %all-gather.2.cloned.1.call-done = bf16[2,1024,16,64]{3,1,2,0:T(8,128)(2,1)} async-done(((bf16[2,1024,4,64]{3,1,2,0:T(8,128)(2,1)}), bf16[2,1024,16,64]{3,1,2,0:T(8,128)(2,1)}) %all-gather.2.cloned.1.call-update) | async-done | bytes 4194320 | tf_op jit(solution)/shard_map/all_gather | solution.py:119
  215.2 8.6 %copy.58 = bf16[2,8,128,16,1,64]{2,5,3,0,1,4:T(8,128)(2,1)} copy(bf16[2,8,128,16,1,64]{5,2,1,3,0,4:T(8,128)(2,1)} %bitcast.98) | data formatting | bytes 8388608 | tf_op jit(solution)/shard_map/reshape | solution.py:68
  223.8 6.5 %copy.59 = bf16[8,2,128,1024]{3,2,1,0:T(8,128)(2,1)} copy(bf16[8,2,128,1024]{2,3,1,0:T(8,128)(2,1)} %bitcast.92) | data formatting | bytes 8388608 | tf_op jit(solution)/shard_map/reshape | solution.py:69
  230.3 5.8 %gather_fusion.2 = bf16[9,2,128,1024]{2,3,1,0:T(8,128)(2,1)} fusion(bf16[8,2,128,1024]{2,3,1,0:T(8,128)(2,1)} %bitcast.93, s32[1024]{0:T(1024)S(1)} %pad_clamp_fusion.1), kind=kCustom, calls=%fused_computation.1.clone | custom fusion | bytes 9437220 | tf_op jit(solution)/shard_map/jit(_take)/gather | solution.py:73
  236.1 5.8 %gather_fusion.1 = bf16[9,2,128,1024]{3,2,1,0:T(8,128)(2,1)} fusion(bf16[8,2,128,1024]{3,2,1,0:T(8,128)(2,1)} %copy.59, s32[1024]{0:T(1024)S(1)} %pad_clamp_fusion.2), kind=kCustom, calls=%fused_computation.clone | custom fusion | bytes 9437220 | tf_op jit(solution)/shard_map/jit(_take)/gather | solution.py:72
  242.0 3.0 %broadcast_select_fusion.1 = bf16[9,2,128,1024]{3,2,1,0:T(8,128)(2,1)S(1)} fusion(bf16[9,2,128,1024]{3,2,1,0:T(8,128)(2,1)} %gather_fusion.1, pred[9]{0:T(512)(128)(4,1)S(1)} %get-tuple-element.13), kind=kLoop, calls=%fused_computation.8 | loop fusion | flops 2359296 | bytes 9437193 | tf_op jit(solution)/shard_map/jit(_take)/select_n | solution.py:72
  246.2 1.5 fusion.20
  247.6 2.0 fusion.21
  (43 shorter events, 7.6 us)
Async XLA Ops:
  7.2 124.6 %copy-start = (bf16[256,2,512]{2,1,0:T(2,128)(2,1)S(1)}, bf16[256,2,512]{2,1,0:T(2,128)(2,1)}, u32[]{:S(2)}) copy-start(bf16[256,2,512]{2,1,0:T(2,128)(2,1)} %param.10) | copy-start | bytes 1572868
  7.2 7.1 %copy-start.4 = (f32[4,4096]{1,0:T(4,128)S(1)}, f32[4,4096]{1,0:T(4,128)}, u32[]{:S(2)}) copy-start(f32[4,4096]{1,0:T(4,128)} %param.8) | copy-start | bytes 196612
  7.2 208.1 %all-gather.2.cloned.1.call-start = ((), (), s32[]{:S(2)}) async-start(), calls=%async_computation.1 | async-start | bytes 10485760 | tf_op jit(solution)/shard_map/all_gather | solution.py:119
  9.1 21.5 %copy-start.3 = (bf16[2,16,4,4096]{3,2,1,0:T(4,128)(2,1)S(1)}, bf16[2,16,4,4096]{3,2,1,0:T(4,128)(2,1)}, u32[]{:S(2)}) copy-start(bf16[2,16,4,4096]{3,2,1,0:T(4,128)(2,1)} %param.7) | copy-start | bytes 3145732
  9.7 20.2 %collective-permute-start = (bf16[2,16,3,4096]{3,1,2,0:T(8,128)(2,1)S(1)}, bf16[2,16,3,4096]{3,1,2,0:T(8,128)(2,1)S(1)}, u32[]{:S(2)}, u32[]{:S(2)}) collective-permute-start(bf16[2,16,3,4096]{3,1,2,0:T(8,128)(2,1)S(1)} %copy.79), channel_id=1, source_target_pairs={{0,64},{64,128},{128,192},{1,65},{65,129},{129,193},{2,66},{66,130... | collective-permute-start | bytes 2359304 | tf_op jit(solution)/shard_map/ppermute | solution.py:20
  120.3 11.4 %copy-start.6 = (s32[256,1]{0,1:T(1,128)S(1)}, s32[256,1]{0,1:T(1,128)}, u32[]{:S(2)}) copy-start(s32[256,1]{0,1:T(1,128)} %param.11) | copy-start | bytes 3076
  131.6 1.8 copy-start.5
  131.6 2.2 copy-start.2
  242.0 3.6 %slice-start = ((s8[4718592]{0:T(1024)(128)(4,1)}), s8[4194304]{0:T(1024)(128)(4,1)S(1)}, s32[]{:S(2)}) async-start(s8[4718592]{0:T(1024)(128)(4,1)} %bitcast.99), calls=%async_computation.2 | async-start | bytes 8388608
  245.0 1.2 slice-start.1
  247.6 3.3 %copy-start.1 = (bf16[256,2,512]{2,1,0:T(2,128)(2,1)S(1)}, bf16[256,2,512]{2,1,0:T(2,128)(2,1)}, u32[]{:S(2)}) copy-start(bf16[256,2,512]{2,1,0:T(2,128)(2,1)} %param.10) | copy-start | bytes 1572868
Sparse Core Ops, SparseCore 0:
  131.8 83.4 all-gather.1
where the time goes:
time: 259 us; the launch traced here: 258 us
  waiting for transfers between devices  90.6 us (35%)
  local copies, waits for them, and re-layouts  85.5 us (33%)
  blocking collectives  41.3 us (16%)
  between operations  14.3 us (6%)
  matrix products  12.9 us (5%)
  other arithmetic  9 us (3%)
  starting transfers between devices  4.11 us (2%)
    all_gather x1, waiting for transfers between devices, shards(): lax.all_gather(shard_piece, 'section', axis=2, tiled=True)  74.9 us
    all_to_all x1, blocking collectives, shards(): lax.all_to_all(spectra, 'chan', split_axis=3, concat_axis=1, tiled=True)  41.3 us
    unnamed x22, local copies, waits for them, and re-layouts  22.1 us
    ppermute x1, waiting for transfers between devices, shifted(): return lax.ppermute(value, axis, pairs)  15.6 us
    convert_element_type x2, local copies, waits for them, and re-layouts, shards(): spectra = channelize(filtered.reshape(2, inputs_dev * frames_dev, NA * NB...  14.2 us
    all_to_all x1, local copies, waits for them, and re-layouts, shards(): lax.all_to_all(spectra, 'chan', split_axis=3, concat_axis=1, tiled=True)  11.4 us
    reshape x1, local copies, waits for them, and re-layouts, pair_products(): spectra.reshape(2, tile_count, TB, frame_count, channel_groups, AVG)  8.56 us
    reshape x1, local copies, waits for them, and re-layouts, pair_products(): jnp.transpose(blocks, (1, 4, 0, 2, 3, 5))  6.46 us
  transfers between devices with their start and end apart: 2, of which 2 were waited for; matrix products, arithmetic and copies ran while one was open for 4% of the time, Pallas kernels for 0%

commit v1 on v0

--- a/solution.py
+++ b/solution.py
@@ -1,3 +1,4 @@
+import functools
 import math
 import jax
 import jax.numpy as jnp
@@ -12,6 +13,42 @@
 TB = 128
 PAIRS = 36
 NBEAM = 256
+
+
+def set_masks_by_axis(original, along_axis):
+    b_now, arr_out, newest = (
+        lax.axis_size(along_axis),
+        lax.axis_index(along_axis),
+        original.shape[2],
+    )
+    shelf = []
+    dev_j = 0
+    while dev_j < b_now:
+        shelf.append((dev_j, (dev_j + 1) % b_now))
+        dev_j += 1
+    pool = []
+    dev_j = 0
+    while dev_j < b_now:
+        pool.append((dev_j, (dev_j - 1) % b_now))
+        dev_j += 1
+    w1 = jnp.zeros((*original.shape[:2], b_now * newest, *original.shape[3:]), original.dtype)
+    w1 = lax.dynamic_update_slice_in_dim(w1, original, arr_out * newest, axis=2)
+    item_now = all_rows = original
+    field_out = b_now // 2
+    b = 1
+    while b < field_out + 1:
+        item_now = lax.ppermute(item_now, perm=shelf, axis_name=along_axis)
+        w1 = lax.dynamic_update_slice_in_dim(w1, item_now, (arr_out - b) % b_now * newest, axis=2)
+        if b < b_now - field_out:
+            all_rows = lax.ppermute(all_rows, axis_name=along_axis, perm=pool)
+            w1 = lax.dynamic_update_slice_in_dim(
+                w1, all_rows, (arr_out + b) % b_now * newest, axis=2
+            )
+        b = b + 1
+    return w1
+
+
+tell_clusters = functools.partial(set_masks_by_axis, along_axis="section")
 
 
 def shifted(value, axis, by):
@@ -116,7 +153,7 @@
     own_items = lax.dynamic_slice_in_dim(
         column_items, lax.axis_index("section") * items_dev, items_dev
     )
-    totals = pair_products(lax.all_gather(shard_piece, "section", axis=2, tiled=True), own_items)
+    totals = pair_products(tell_clusters(shard_piece), own_items)
     visibility = (totals * mean_factor)[None]
     return (visibility, beam_power)
 

time: 259 us -> 224 us (0.86)
  waiting for transfers between devices: 90.6 us -> 53.3 us
  between operations: 14.3 us -> 0.99 us
  local copies, waits for them, and re-layouts: 85.5 us -> 92.7 us
  starting transfers between devices: 4.11 us -> 7.78 us
  matrix products: 12.9 us -> 15.6 us
    all_gather x1 -> x0, waiting for transfers between devices: 74.9 us -> none  [shards(): lax.all_gather(shard_piece, 'section', axis=2, tiled=True)]
    ppermute x0 -> x3, waiting for transfers between devices: none -> 37.7 us  [the longest x2 37.7 us: set_masks_by_axis(): item_now = lax.ppermute(item_now, perm=shelf, axis_name=along_axis)]
    reshape x1 -> x0, local copies, waits for them, and re-layouts: 8.56 us -> none  [pair_products(): spectra.reshape(2, tile_count, TB, frame_count, channel_groups, AVG)]
    transpose x0 -> x1, local copies, waits for them, and re-layouts: none -> 5.41 us  [pair_products(): jnp.transpose(blocks, (1, 4, 0, 2, 3, 5))]
    unnamed x22 -> x27, local copies, waits for them, and re-layouts: 22.1 us -> 26.6 us
    dynamic_update_slice x0 -> x4, local copies, waits for them, and re-layouts: none -> 4.03 us  [the longest x2 2.62 us: set_masks_by_axis(): lax.dynamic_update_slice_in_dim(w1, item_now, (arr_out - b) % b_now * new...]
    dot_general x1, matrix products: 1.46 us -> 5.35 us  [pair_products(): lax.dot_general(row_block, col_block, numbers, preferred_element_type=jnp...]
    ppermute x0 -> x3, starting transfers between devices: none -> 3.71 us  [the longest x2 2.21 us: set_masks_by_axis(): item_now = lax.ppermute(item_now, perm=shelf, axis_name=along_axis)]
  transfers between devices with their start and end apart: 2 -> 4, of which waited for: 2 -> 3; matrix products, arithmetic and copies ran while one was open for 4% -> 5% of each run, Pallas kernels for 0% -> 0%
where the time goes in v1:
time: 224 us; the launch traced here: 222 us
  local copies, waits for them, and re-layouts  92.7 us (41%)
  waiting for transfers between devices  53.3 us (24%)
  blocking collectives  41.3 us (18%)
  matrix products  15.6 us (7%)
  other arithmetic  10.5 us (5%)
  starting transfers between devices  7.78 us (3%)
    all_to_all x1, blocking collectives, shards(): lax.all_to_all(spectra, 'chan', split_axis=3, concat_axis=1, tiled=True)  41.3 us
    ppermute x2, waiting for transfers between devices, set_masks_by_axis(): item_now = lax.ppermute(item_now, perm=shelf, axis_name=along_axis)  37.7 us
    unnamed x27, local copies, waits for them, and re-layouts  26.6 us
    ppermute x1, waiting for transfers between devices, shifted(): return lax.ppermute(value, axis, pairs)  15.6 us
    convert_element_type x2, local copies, waits for them, and re-layouts, shards(): spectra = channelize(filtered.reshape(2, inputs_dev * frames_dev, NA * NB...  14.2 us
    all_to_all x2, local copies, waits for them, and re-layouts, shards(): lax.all_to_all(spectra, 'chan', split_axis=3, concat_axis=1, tiled=True)  12.2 us
    reshape x1, local copies, waits for them, and re-layouts, pair_products(): jnp.transpose(blocks, (1, 4, 0, 2, 3, 5))  6.77 us
    gather x1, local copies, waits for them, and re-layouts, pair_products(): jnp.take(tile_table, col_tiles * channel_groups + local_channel, axis=0)  5.92 us
  transfers between devices with their start and end apart: 4, of which 3 were waited for; matrix products, arithmetic and copies ran while one was open for 5% of the time, Pallas kernels for 0%

profile of v1, /device:TPU:1, one launch (start us, length us, event | category | flops | bytes accessed | tf_op | source)
XLA Modules:
  0.0 222.1 jit_solution(4254572561794098069)
XLA Ops:
  0.7 2.0 slice.54
  3.2 4.1 %collective-permute-start = (bf16[2,16,3,4096]{3,1,2,0:T(8,128)(2,1)S(1)}, bf16[2,16,3,4096]{3,1,2,0:T(8,128)(2,1)S(1)}, u32[]{:S(2)}, u32[]{:S(2)}) collective-permute-start(bf16[2,16,3,4096]{3,1,2,0:T(8,128)(2,1)S(1)} %copy.89), channel_id=1, source_target_pairs={{0,64},{64,128},{128,192},{1,65},{65,129},{129,193},{2,66},{66,130... | collective-permute-start | bytes 2359304 | tf_op jit(solution)/shard_map/ppermute | solution.py:57
  7.8 15.6 %collective-permute-done = bf16[2,16,3,4096]{3,1,2,0:T(8,128)(2,1)S(1)} collective-permute-done((bf16[2,16,3,4096]{3,1,2,0:T(8,128)(2,1)S(1)}, bf16[2,16,3,4096]{3,1,2,0:T(8,128)(2,1)S(1)}, u32[]{:S(2)}, u32[]{:S(2)}) %collective-permute-start) | collective-permute-done | bytes 786464 | tf_op jit(solution)/shard_map/ppermute | solution.py:57
  27.0 3.3 %reshape_reshape.4 = f32[2,64,64,64]{3,2,1,0:T(8,128)} reshape(f32[2,16,4,4096]{3,2,1,0:T(4,128)S(1)} %fusion.14) | data formatting | bytes 4194304 | tf_op jit(solution)/shard_map/reshape;reshape | solution.py:72
  30.4 4.2 %fusion.10 = f32[2,64,64,64]{3,2,1,0:T(8,128)S(1)} fusion(f32[2,64,64,64]{3,2,1,0:T(8,128)} %reshape_reshape.4, f32[1,2,64,64]{2,3,0,1:T(8,128)S(1)} %get-tuple-element.27, f32[1,2,64,64]{2,3,0,1:T(8,128)S(1)} %get-tuple-element.26), kind=kOutput, calls=%fused_computation.18 | convolution fusion | flops 402669568 | bytes 4259840 | tf_op jit(solution)/shard_map/qmab,qrac->rmcb/dot_general | solution.py:73
  35.5 3.3 %fusion.13 = bf16[2,64,64,64]{3,2,1,0:T(8,128)(2,1)S(1)} fusion(f32[1,2,64,64]{2,3,0,1:T(8,128)S(1)} %get-tuple-element.27, f32[1,2,64,64]{2,3,0,1:T(8,128)S(1)} %get-tuple-element.26, f32[1,64,64,64]{3,2,1,0:T(8,128)S(1)} %get-tuple-element.21, f32[1,64,64,64]{3,2,1,0:T(8,128)S(1)} %get-tuple-element.20), kind=kOutput, calls=%fused_computation.19 | convolution fusion | flops 403718144 | bytes 3211264 | tf_op jit(solution)/shard_map/rmcb,rsbd->smdc/dot_general | solution.py:87
  38.8 2.2 convert_element_type.61
  41.0 12.0 %copy.61 = bf16[2,16,4,4096]{1,2,0,3:T(4,128)(2,1)} copy(bf16[2,16,4,4096]{3,2,1,0:T(4,128)(2,1)} %convert_element_type.61) | data formatting | bytes 2097152 | tf_op jit(solution)/shard_map/convert_element_type | solution.py:134
  53.0 11.9 %reshape.317 = bf16[64,2,4096]{2,1,0:T(2,128)(2,1)S(1)} reshape(bf16[4096,2,4,16]{3,2,1,0:T(4,128)(2,1)} %bitcast.104) | data formatting | bytes 2097152
  64.9 41.3 %all_to_all.18 = bf16[64,2,4096]{2,1,0:T(2,128)(2,1)S(1)} all-to-all(bf16[64,2,4096]{2,1,0:T(2,128)(2,1)S(1)} %reshape.317), channel_id=1, replica_groups=mesh['section'=4,'chan'=64] {'chan'}, dimensions={0} | all-to-all | bytes 2097152 | tf_op jit(solution)/shard_map/all_to_all | solution.py:138
  106.2 7.5 %reshape.318 = bf16[4096,2,4,16]{3,2,1,0:T(4,128)(2,1)} reshape(bf16[64,2,4096]{2,1,0:T(2,128)(2,1)S(1)} %all_to_all.18) | data formatting | bytes 2097152
  113.8 10.6 %copy.84 = bf16[2,16,4,64,64]{4,1,3,2,0:T(8,128)(2,1)S(1)} copy(bf16[2,16,4,64,64]{1,2,0,4,3:T(4,128)(2,1)} %bitcast.103) | data formatting | bytes 2097152 | tf_op jit(solution)/shard_map/all_to_all | solution.py:138
  126.0 2.2 collective-permute-start.1
  130.1 23.3 %collective-permute-done.1 = bf16[2,1024,4,64]{1,3,2,0:T(8,128)(2,1)} collective-permute-done((bf16[2,1024,4,64]{1,3,2,0:T(8,128)(2,1)}, bf16[2,1024,4,64]{1,3,2,0:T(8,128)(2,1)}, u32[]{:S(2)}, u32[]{:S(2)}) %collective-permute-start.1) | collective-permute-done | bytes 1048608 | tf_op jit(solution)/shard_map/ppermute | solution.py:40
  155.3 3.5 %copy.73 = bf16[2,512,2,4,64]{1,4,3,2,0:T(8,128)(2,1)} copy(bf16[2,512,2,4,64]{4,2,1,3,0:T(2,128)(2,1)S(1)} %bitcast.107) | data formatting | bytes 2097152 | tf_op jit(solution)/shard_map/reshape.8
  164.6 14.4 %collective-permute-done.3 = bf16[2,1024,4,64]{1,3,2,0:T(8,128)(2,1)} collective-permute-done((bf16[2,1024,4,64]{1,3,2,0:T(8,128)(2,1)}, bf16[2,1024,4,64]{1,3,2,0:T(8,128)(2,1)}, u32[]{:S(2)}, u32[]{:S(2)}) %collective-permute-start.3) | collective-permute-done | bytes 1048608 | tf_op jit(solution)/shard_map/ppermute | solution.py:40
  180.3 3.0 %copy.90 = bf16[256,8,8,128]{3,2,1,0:T(8,128)(2,1)} copy(bf16[256,8,8,128]{3,1,2,0:T(8,128)(2,1)S(1)} %bitcast.108) | data formatting | bytes 8388608
  183.4 6.8 %copy.68 = bf16[8,2,128,1024]{3,2,1,0:T(8,128)(2,1)} copy(bf16[8,2,128,1024]{2,0,3,1:T(8,128)(2,1)} %bitcast.101) | data formatting | bytes 8388608 | tf_op jit(solution)/shard_map/reshape | solution.py:106
  190.1 5.4 %copy.67 = bf16[8,1,2,128,16,64]{3,5,4,2,0,1:T(8,128)(2,1)} copy(bf16[8,1,2,128,16,64]{3,0,5,4,2,1:T(8,128)(2,1)} %bitcast.102) | data formatting | bytes 8388608 | tf_op jit(solution)/shard_map/transpose | solution.py:106
  195.5 5.8 %gather_fusion.1 = bf16[9,2,128,1024]{3,2,1,0:T(8,128)(2,1)} fusion(bf16[8,2,128,1024]{3,2,1,0:T(8,128)(2,1)} %copy.68, s32[1024]{0:T(1024)S(1)} %pad_clamp_fusion.2), kind=kCustom, calls=%fused_computation.clone | custom fusion | bytes 9437220 | tf_op jit(solution)/shard_map/jit(_take)/gather | solution.py:109
  201.3 2.9 %broadcast_select_fusion.1 = bf16[9,2,128,1024]{3,2,1,0:T(8,128)(2,1)S(1)} fusion(bf16[9,2,128,1024]{3,2,1,0:T(8,128)(2,1)} %gather_fusion.1, pred[9]{0:T(512)(128)(4,1)S(1)} %get-tuple-element.13), kind=kLoop, calls=%fused_computation.8 | loop fusion | flops 2359296 | bytes 9437193 | tf_op jit(solution)/shard_map/jit(_take)/select_n | solution.py:109
  207.0 5.9 %gather_fusion.2 = bf16[9,2,128,1024]{2,3,1,0:T(8,128)(2,1)} fusion(bf16[8,2,128,1024]{2,3,1,0:T(8,128)(2,1)} %bitcast.105, s32[1024]{0:T(1024)S(1)} %pad_clamp_fusion.1), kind=kCustom, calls=%fused_computation.1.clone | custom fusion | bytes 9437220 | tf_op jit(solution)/shard_map/jit(_take)/gather | solution.py:110
  213.0 5.4 %fusion.20 = f32[1,9,1,128,128]{4,3,1,2,0:T(8,128)S(1)} fusion(bf16[9,2,128,1024]{3,2,1,0:T(8,128)(2,1)} %copy-done.2, bf16[9,2,128,1024]{2,3,1,0:T(8,128)(2,1)} %gather_fusion.2, pred[9]{0:T(512)(128)(4,1)S(1)} %get-tuple-element.16), kind=kOutput, calls=%fused_computation.32 | convolution fusion | flops 606339072 | bytes 10027017 | tf_op jit(solution)/shard_map/dot_general | solution.py:113
  218.8 2.0 fusion.21
  (56 shorter events, 22.6 us)
Async XLA Ops:
  0.6 152.9 %copy-start = (bf16[256,2,512]{2,1,0:T(2,128)(2,1)S(1)}, bf16[256,2,512]{2,1,0:T(2,128)(2,1)}, u32[]{:S(2)}) copy-start(bf16[256,2,512]{2,1,0:T(2,128)(2,1)} %param.10) | copy-start | bytes 1572868
  0.6 23.5 %copy-start.6 = (bf16[2,16,4,4096]{3,2,1,0:T(4,128)(2,1)S(1)}, bf16[2,16,4,4096]{3,2,1,0:T(4,128)(2,1)}, u32[]{:S(2)}) copy-start(bf16[2,16,4,4096]{3,2,1,0:T(4,128)(2,1)} %param.7) | copy-start | bytes 3145732
  0.7 7.1 %copy-start.8 = (f32[4,4096]{1,0:T(4,128)S(1)}, f32[4,4096]{1,0:T(4,128)}, u32[]{:S(2)}) copy-start(f32[4,4096]{1,0:T(4,128)} %param.8) | copy-start | bytes 196612
  3.2 20.2 %collective-permute-start = (bf16[2,16,3,4096]{3,1,2,0:T(8,128)(2,1)S(1)}, bf16[2,16,3,4096]{3,1,2,0:T(8,128)(2,1)S(1)}, u32[]{:S(2)}, u32[]{:S(2)}) collective-permute-start(bf16[2,16,3,4096]{3,1,2,0:T(8,128)(2,1)S(1)} %copy.89), channel_id=1, source_target_pairs={{0,64},{64,128},{128,192},{1,65},{65,129},{129,193},{2,66},{66,130... | collective-permute-start | bytes 2359304 | tf_op jit(solution)/shard_map/ppermute | solution.py:57
  113.8 14.5 %copy-start.9 = (s32[1,36]{1,0:T(1,128)S(1)}, s32[1,36]{1,0:T(1,128)}, u32[]{:S(2)}) copy-start(s32[1,36]{1,0:T(1,128)} %param.9) | copy-start | bytes 436
  113.8 14.6 %copy-start.10 = (s32[256,1]{0,1:T(1,128)S(1)}, s32[256,1]{0,1:T(1,128)}, u32[]{:S(2)}) copy-start(s32[256,1]{0,1:T(1,128)} %param.11) | copy-start | bytes 3076
  126.0 27.4 %collective-permute-start.1 = (bf16[2,1024,4,64]{1,3,2,0:T(8,128)(2,1)}, bf16[2,1024,4,64]{1,3,2,0:T(8,128)(2,1)}, u32[]{:S(2)}, u32[]{:S(2)}) collective-permute-start(bf16[2,1024,4,64]{1,3,2,0:T(8,128)(2,1)} %copy.64), channel_id=1, source_target_pairs={{0,64},{64,128},{128,192},{192,0},{1,65},{65,129},{129,193},{193,1... | collective-permute-start | bytes 3145736 | tf_op jit(solution)/shard_map/ppermute | solution.py:40
  128.6 34.7 %collective-permute-start.2 = (bf16[2,1024,4,64]{1,3,2,0:T(8,128)(2,1)}, bf16[2,1024,4,64]{1,3,2,0:T(8,128)(2,1)}, u32[]{:S(2)}, u32[]{:S(2)}) collective-permute-start(bf16[2,1024,4,64]{1,3,2,0:T(8,128)(2,1)} %copy.64), channel_id=1, source_target_pairs={{0,192},{64,0},{128,64},{192,128},{1,193},{65,1},{129,65},{193,129... | collective-permute-start | bytes 3145736 | tf_op jit(solution)/shard_map/ppermute | solution.py:43
  153.4 25.6 %collective-permute-start.3 = (bf16[2,1024,4,64]{1,3,2,0:T(8,128)(2,1)}, bf16[2,1024,4,64]{1,3,2,0:T(8,128)(2,1)}, u32[]{:S(2)}, u32[]{:S(2)}) collective-permute-start(bf16[2,1024,4,64]{1,3,2,0:T(8,128)(2,1)} %collective-permute-done.1), channel_id=1, source_target_pairs={{0,64},{64,128},{128,192},{192,0},{1,65},{65,129},{129,193},{193,1... | collective-permute-start | bytes 3145736 | tf_op jit(solution)/shard_map/ppermute | solution.py:40
  158.7 1.2 copy-start.5
  158.7 1.5 copy-start.4
  204.2 2.9 %copy-start.2 = (bf16[9,2,128,1024]{3,2,1,0:T(8,128)(2,1)}, bf16[9,2,128,1024]{3,2,1,0:T(8,128)(2,1)S(1)}, u32[]{:S(2)}) copy-start(bf16[9,2,128,1024]{3,2,1,0:T(8,128)(2,1)S(1)} %broadcast_select_fusion.1) | copy-start | bytes 14155780
  213.0 5.4 %copy-start.3 = (bf16[9,2,128,1024]{2,3,1,0:T(8,128)(2,1)S(1)}, bf16[9,2,128,1024]{2,3,1,0:T(8,128)(2,1)}, u32[]{:S(2)}) copy-start(bf16[9,2,128,1024]{2,3,1,0:T(8,128)(2,1)} %gather_fusion.2) | copy-start | bytes 14155780
  213.0 5.9 %copy-start.7 = (bf16[9,1,128,1024]{3,2,1,0:T(8,128)(2,1)S(1)}, bf16[9,1,128,1024]{3,2,1,0:T(8,128)(2,1)}, u32[]{:S(2)}) copy-start(bf16[9,1,128,1024]{3,2,1,0:T(8,128)(2,1)} %get-tuple-element.19) | copy-start | bytes 7077892
  218.8 3.2 %copy-start.1 = (bf16[256,2,512]{2,1,0:T(2,128)(2,1)S(1)}, bf16[256,2,512]{2,1,0:T(2,128)(2,1)}, u32[]{:S(2)}) copy-start(bf16[256,2,512]{2,1,0:T(2,128)(2,1)} %param.10) | copy-start | bytes 1572868
